TPU v7x, 32 devices: a whole 2x2x4 slice. The times are simulated.
32 devices in a mesh: grp: 2 (over x), samp: 16 (over z, y, core).
Axes of the slice: x: 2, y: 2, z: 4, core: 2. Of those that a mesh axis runs over, the one named last changes fastest.
Arguments:
- genotypes: int32 [32768, 2048], P(('grp', 'samp')), parts along dimension 0, may hold values from 0 to 2
- probe_signs: int32 [32, 32768], P(None, ('grp', 'samp')), parts along dimension 1, may hold values from 0 to 1
- phenotype: float32 [32768], P(('grp', 'samp')), parts along dimension 0, may hold values from -6 to 6
- marker_mean: float32 [2048], replicated, may hold values from 0.2 to 1.8
- marker_scale: float32 [2048], replicated, may hold values from 0.5 to 4
- marker_bin: int32 [2048], replicated, may hold values from 0 to 15, as said below
Outputs:
- products: float32 [16, 33, 32768], P(None, None, ('grp', 'samp')), parts along dimension 2
- gram: float32 [32, 16, 33], P('grp'), parts along dimension 0
There are 2 independent parts, one for each index of `grp`. A program takes and returns all parts, laid end to end along the dimension named above; an argument that names none is the same for every part. Nothing has to cross between parts.
Inputs may be any that keep to these rules, and one draw needn't show every extreme that they name: `marker_bin`: every bin holds exactly 128 markers.
All inputs are finite; a program needn't handle non-finite values.
Results may differ from a plain program's by a relative error of at most 0.0001.
Values sent between devices are 32-bit elements; how exact they have to be, the bound alone decides.
A program may use at most 128 MiB of HBM per device.

v0:
```python
import jax
import jax.numpy as jnp
from jax import lax
from jax.sharding import PartitionSpec as P

BINS = 16
M_BIN = 128


def shards(genotypes, probe_signs, phenotype, marker_mean, marker_scale, marker_bin):
    samples = genotypes.shape[0]
    devices = lax.axis_size("samp")
    total = jnp.float32(samples * devices)
    order = jnp.argsort(marker_bin, stable=True)
    picked = jnp.take(genotypes, order, axis=1).astype(jnp.float32)
    standard = (picked - marker_mean[order]) * marker_scale[order]
    vectors = jnp.concatenate(
        [(2 * probe_signs - 1).astype(jnp.float32), phenotype[None, :]], axis=0
    )
    share = lax.psum_scatter(
        jnp.dot(
            standard.T,
            vectors.T,
            precision=lax.Precision.HIGHEST,
            preferred_element_type=jnp.float32,
        ),
        "samp",
        scatter_dimension=0,
        tiled=True,
    )
    scores = lax.all_gather(share, "samp", axis=0, tiled=True)
    scores = scores / jnp.sqrt(total)
    blocks = standard.reshape(samples, BINS, M_BIN)
    weights = scores.reshape(BINS, M_BIN, scores.shape[1])
    products = jnp.einsum(
        "skm,kmr->krs", blocks, weights, precision=lax.Precision.HIGHEST
    ) / jnp.sqrt(jnp.float32(M_BIN))
    local_gram = jnp.einsum("krs,lrs->klr", products, products, precision=lax.Precision.HIGHEST)
    gram = lax.psum(local_gram, "samp") / total
    return (products, gram)


def solution(mesh):
    in_specs = (
        P(("grp", "samp"), None),
        P(None, ("grp", "samp")),
        P(("grp", "samp")),
        P(),
        P(),
        P(),
    )
    out_specs = (P(None, None, ("grp", "samp")), P("grp", None, None))
    return jax.shard_map(shards, mesh=mesh, in_specs=in_specs, out_specs=out_specs, check_vma=False)
```

profile of v0, /device:TPU:0, one launch (start us, length us, event | category | flops | bytes accessed | tf_op | source)
XLA Modules:
  0.0 233.8 jit_solution(9177498620670587703)
XLA Ops:
  7.2 0.0 copy-start
  7.2 0.0 copy-start.1
  7.2 0.0 reduce-scatter.2.cloned.1.call-start
  7.2 5.7 %sort.17 = (s32[2048]{0:T(1024)}, s32[2048]{0:T(1024)S(1)}) sort(s32[2048]{0:T(1024)} %param.11, s32[2048]{0:T(1024)S(1)} %iota.4), dimensions={0}, to_apply=%region_0.0 | sort | flops 22528 | bytes 32768 | tf_op jit(solution)/shard_map/jit(argsort)/sort | solution.py:14
  13.0 0.0 copy-done
  13.0 0.0 copy-start.3
  13.0 11.8 %gather_fusion.2 = f32[2048]{0:T(1024)S(1)} fusion(f32[2048]{0:T(1024)S(1)} %copy-done, s32[2048]{0:T(1024)S(1)} %fusion.25), kind=kCustom, calls=%fused_computation.2 | custom fusion | bytes 24576 | tf_op jit(solution)/shard_map/gather | solution.py:16
  24.8 0.0 copy-done.1
  24.8 11.8 %gather_fusion.1 = f32[2048]{0:T(1024)S(1)} fusion(f32[2048]{0:T(1024)S(1)} %copy-done.1, s32[2048]{0:T(1024)S(1)} %fusion.25), kind=kCustom, calls=%fused_computation.1 | custom fusion | bytes 24576 | tf_op jit(solution)/shard_map/gather | solution.py:16
  36.6 0.0 copy-done.3
  36.6 9.3 %copy.15 = s32[1024,2048]{0,1:T(8,128)} copy(s32[1024,2048]{1,0:T(8,128)} %param.6) | data formatting | bytes 16777216 | tf_op args[0]
  45.9 0.0 copy-start.4
  45.9 15.1 %gather_fusion = s32[2048,1024]{1,0:T(8,128)} fusion(s32[1024,2048]{0,1:T(8,128)} %copy.15, s32[2048]{0:T(1024)S(1)} %fusion.25), kind=kCustom, calls=%fused_computation | custom fusion | bytes 16785408 | tf_op jit(solution)/shard_map/jit(_take)/gather | solution.py:15
  61.1 0.0 copy-done.4
  61.1 12.3 %fusion.3 = f32[2048,33]{0,1:T(8,128)} fusion(s32[2048,1024]{1,0:T(8,128)} %gather_fusion, f32[2048]{0:T(1024)S(1)} %gather_fusion.2, f32[2048]{0:T(1024)S(1)} %gather_fusion.1, pred[2048]{0:T(1024)(128)(4,1)S(1)} %compare_and_fusion, f32[1,1024]{1,0:T(1,128)S(1)} %bitcast.31, f32[32,1024]{1,0:T(8,128)S(1)} %add_convert_fusion), kind=kOutput, calls=%fused_computation.7 | convolution fusion | flops 838894592 | bytes 8812544 | tf_op jit(solution)/shard_map/dot_general | solution.py:21
  73.3 0.0 reduce-scatter.2.cloned.1.call-update
  73.4 9.3 %copy.16 = s32[1024,16,128]{2,0,1:T(8,128)} copy(s32[1024,16,128]{0,2,1:T(8,128)} %bitcast.26) | data formatting | bytes 16777216 | tf_op jit(solution)/shard_map/jit(_take)/gather | solution.py:15
  82.6 45.9 %reduce-scatter.2.cloned.1.call-done = f32[128,33]{0,1:T(8,128)} async-done(((f32[2048,33]{0,1:T(8,128)}), f32[128,33]{0,1:T(8,128)}) %reduce-scatter.2.cloned.1.call-update) | async-done | bytes 16912 | tf_op jit(solution)/shard_map/reduce_scatter | solution.py:20
  128.6 20.7 %all_gather.3 = f32[2048,33]{0,1:T(8,128)S(1)} all-gather(f32[128,33]{0,1:T(8,128)} %reduce-scatter.2.cloned.1.call-done), channel_id=1, replica_groups=mesh['grp'=2,'samp'=16] {'samp'}, dimensions={0}, use_global_device_ids=true | all-gather | bytes 287232 | tf_op jit(solution)/shard_map/all_gather | solution.py:31
  149.3 0.1 copy.22
  149.4 11.3 %fusion.18 = f32[16,33,1024]{2,1,0:T(8,128)S(1)} fusion(s32[1024,16,128]{2,0,1:T(8,128)} %copy.16, f32[16,128]{1,0:T(8,128)S(1)} %bitcast.29, f32[16,128]{1,0:T(8,128)S(1)} %bitcast.30, pred[16,128]{1,0:T(8,128)(4,1)S(1)} %fusion.31, f32[16,128,33]{1,0,2:T(8,128)S(1)} %slice_bitcast_fusion), kind=kOutput, calls=%fused_computation.21 | convolution fusion | flops 839401472 | bytes 10840064 | tf_op jit(solution)/shard_map/skm,kmr->krs/dot_general | solution.py:35
  160.7 1.3 copy.20
  161.9 0.0 copy-start.2
  162.0 3.1 %convolution_bitcast_fusion = f32[16,16,33]{0,1,2:T(8,128)S(1)} fusion(f32[16,33,1024]{2,0,1:T(8,128)S(1)} %copy.20), kind=kOutput, calls=%fused_computation.22 | convolution fusion | flops 103809024 | bytes 2196480 | tf_op jit(solution)/shard_map/krs,lrs->klr/dot_general | solution.py:38
  165.1 61.0 %psum.7 = f32[16,16,33]{0,1,2:T(8,128)S(1)} all-reduce(f32[16,16,33]{0,1,2:T(8,128)S(1)} %convolution_bitcast_fusion), channel_id=1, replica_groups=mesh['grp'=2,'samp'=16] {'samp'}, use_global_device_ids=true, to_apply=%region_2.3 | all-reduce | flops 8448 | bytes 67584 | tf_op jit(solution)/shard_map/psum | solution.py:39
  226.1 0.8 copy.21
  227.0 0.0 copy-done.2
  (8 shorter events, 0.1 us)
Async XLA Ops:
  7.2 5.8 %copy-start = (f32[2048]{0:T(1024)S(1)}, f32[2048]{0:T(1024)}, u32[]{:S(2)}) copy-start(f32[2048]{0:T(1024)} %param.10) | copy-start | bytes 24580
  7.2 17.6 %copy-start.1 = (f32[2048]{0:T(1024)S(1)}, f32[2048]{0:T(1024)}, u32[]{:S(2)}) copy-start(f32[2048]{0:T(1024)} %param.9) | copy-start | bytes 24580
  7.2 121.4 %reduce-scatter.2.cloned.1.call-start = ((), (), s32[]{:S(2)}) async-start(), calls=%async_computation.1 | async-start | bytes 348160 | tf_op jit(solution)/shard_map/reduce_scatter | solution.py:20
  13.0 23.6 %copy-start.3 = (s32[32,1024]{1,0:T(8,128)S(1)}, s32[32,1024]{1,0:T(8,128)}, u32[]{:S(2)}) copy-start(s32[32,1024]{1,0:T(8,128)} %param.7) | copy-start | bytes 393220
  45.9 15.2 %copy-start.4 = (f32[1024]{0:T(1024)S(1)}, f32[1024]{0:T(1024)}, u32[]{:S(2)}) copy-start(f32[1024]{0:T(1024)} %param.8) | copy-start | bytes 12292
  161.9 65.0 %copy-start.2 = (f32[16,33,1024]{2,0,1:T(8,128)}, f32[16,33,1024]{2,0,1:T(8,128)S(1)}, u32[]{:S(2)}) copy-start(f32[16,33,1024]{2,0,1:T(8,128)S(1)} %copy.20) | copy-start | bytes 6488068
Sparse Core Ops, SparseCore 0:
  73.5 55.0 reduce-scatter.1
where the time goes:
time: 234 us
  blocking collectives  81.7 us (35%)
  local copies, waits for them, and re-layouts  59.5 us (25%)
  waiting for transfers between devices  45.9 us (20%)
  matrix products  26.7 us (11%)
  between operations  14.2 us (6%)
  other arithmetic  5.82 us (2%)
    psum x1, blocking collectives, shards(): gram = lax.psum(local_gram, 'samp') / total  61 us
    reduce_scatter x1, waiting for transfers between devices, shards(): lax.psum_scatter(jnp.dot(standard.T, vectors.T, precision=lax.Precision.H...  45.9 us
    gather x2, local copies, waits for them, and re-layouts, shards(): picked = jnp.take(genotypes, order, axis=1).astype(jnp.float32)  24.4 us
    gather x2, local copies, waits for them, and re-layouts, shards(): standard = (picked - marker_mean[order]) * marker_scale[order]  23.6 us
    all_gather x1, blocking collectives, shards(): scores = lax.all_gather(share, 'samp', axis=0, tiled=True)  20.7 us
    dot_general x1, matrix products, shards(): jnp.dot(standard.T, vectors.T, precision=lax.Precision.HIGHEST, preferred...  12.3 us
    unnamed x14, local copies, waits for them, and re-layouts  11.5 us
    dot_general x1, matrix products, shards(): jnp.einsum('skm,kmr->krs', blocks, weights, precision=lax.Precision.HIGHEST)  11.3 us
  transfers between devices with their start and end apart: 1, of which 1 were waited for; matrix products, arithmetic and copies ran while one was open for 4% of the time, Pallas kernels for 0%

commit v1 on v0

--- a/solution.py
+++ b/solution.py
@@ -1,3 +1,4 @@
+import functools
 import jax
 import jax.numpy as jnp
 from jax import lax
@@ -5,6 +6,13 @@
 
 BINS = 16
 M_BIN = 128
+
+
+def edit_the_types(arr_in, bus_axis):
+    return jnp.sum(jax.lax.all_gather(arr_in, bus_axis), axis=0)
+
+
+records_fix = functools.partial(edit_the_types, bus_axis="samp")
 
 
 def shards(genotypes, probe_signs, phenotype, marker_mean, marker_scale, marker_bin):
@@ -36,7 +44,7 @@
         "skm,kmr->krs", blocks, weights, precision=lax.Precision.HIGHEST
     ) / jnp.sqrt(jnp.float32(M_BIN))
     local_gram = jnp.einsum("krs,lrs->klr", products, products, precision=lax.Precision.HIGHEST)
-    gram = lax.psum(local_gram, "samp") / total
+    gram = records_fix(local_gram) / total
     return (products, gram)
 
 

time: 234 us -> 205 us (0.88)
  blocking collectives: 81.7 us -> 50.3 us
  other arithmetic: 5.82 us -> 8.21 us
    psum x1 -> x0, blocking collectives: 61 us -> none  [shards(): gram = lax.psum(local_gram, 'samp') / total]
    all_gather x0 -> x1, blocking collectives: none -> 29.5 us  [edit_the_types(): return jnp.sum(jax.lax.all_gather(arr_in, bus_axis), axis=0)]
    unnamed x14 -> x13, local copies, waits for them, and re-layouts: 11.5 us -> 10.6 us
  transfers between devices with their start and end apart: 1 -> 1, of which waited for: 1 -> 1; matrix products, arithmetic and copies ran while one was open for 4% -> 5% of each run, Pallas kernels for 0% -> 0%
where the time goes in v1:
time: 205 us; the launch traced here: 204 us
  local copies, waits for them, and re-layouts  58.8 us (29%)
  blocking collectives  50.3 us (25%)
  waiting for transfers between devices  45.9 us (22%)
  matrix products  26.7 us (13%)
  between operations  14.2 us (7%)
  other arithmetic  8.21 us (4%)
    reduce_scatter x1, waiting for transfers between devices, shards(): lax.psum_scatter(jnp.dot(standard.T, vectors.T, precision=lax.Precision.H...  45.9 us
    all_gather x1, blocking collectives, edit_the_types(): return jnp.sum(jax.lax.all_gather(arr_in, bus_axis), axis=0)  29.5 us
    gather x2, local copies, waits for them, and re-layouts, shards(): picked = jnp.take(genotypes, order, axis=1).astype(jnp.float32)  24.4 us
    gather x2, local copies, waits for them, and re-layouts, shards(): standard = (picked - marker_mean[order]) * marker_scale[order]  23.6 us
    all_gather x1, blocking collectives, shards(): scores = lax.all_gather(share, 'samp', axis=0, tiled=True)  20.7 us
    dot_general x1, matrix products, shards(): jnp.dot(standard.T, vectors.T, precision=lax.Precision.HIGHEST, preferred...  12.3 us
    dot_general x1, matrix products, shards(): jnp.einsum('skm,kmr->krs', blocks, weights, precision=lax.Precision.HIGHEST)  11.3 us
    unnamed x13, local copies, waits for them, and re-layouts  10.6 us
  transfers between devices with their start and end apart: 1, of which 1 were waited for; matrix products, arithmetic and copies ran while one was open for 5% of the time, Pallas kernels for 0%

profile of v1, /device:TPU:0, one launch (start us, length us, event | category | flops | bytes accessed | tf_op | source)
XLA Modules:
  0.0 204.1 jit_solution(6415326989422621162)
XLA Ops:
  7.2 0.0 copy-start
  7.2 0.0 copy-start.1
  7.2 0.0 reduce-scatter.2.cloned.1.call-start
  7.2 5.7 %sort.17 = (s32[2048]{0:T(1024)}, s32[2048]{0:T(1024)S(1)}) sort(s32[2048]{0:T(1024)} %param.11, s32[2048]{0:T(1024)S(1)} %iota.4), dimensions={0}, to_apply=%region_0.0 | sort | flops 22528 | bytes 32768 | tf_op jit(solution)/shard_map/jit(argsort)/sort | solution.py:22
  13.0 0.0 copy-done
  13.0 0.0 copy-start.3
  13.0 11.8 %gather_fusion.2 = f32[2048]{0:T(1024)S(1)} fusion(f32[2048]{0:T(1024)S(1)} %copy-done, s32[2048]{0:T(1024)S(1)} %fusion.25), kind=kCustom, calls=%fused_computation.2 | custom fusion | bytes 24576 | tf_op jit(solution)/shard_map/gather | solution.py:24
  24.8 0.0 copy-done.1
  24.8 11.8 %gather_fusion.1 = f32[2048]{0:T(1024)S(1)} fusion(f32[2048]{0:T(1024)S(1)} %copy-done.1, s32[2048]{0:T(1024)S(1)} %fusion.25), kind=kCustom, calls=%fused_computation.1 | custom fusion | bytes 24576 | tf_op jit(solution)/shard_map/gather | solution.py:24
  36.6 0.0 copy-done.3
  36.6 9.3 %copy.21 = s32[1024,2048]{0,1:T(8,128)} copy(s32[1024,2048]{1,0:T(8,128)} %param.6) | data formatting | bytes 16777216 | tf_op args[0]
  45.9 0.0 copy-start.4
  45.9 15.1 %gather_fusion = s32[2048,1024]{1,0:T(8,128)} fusion(s32[1024,2048]{0,1:T(8,128)} %copy.21, s32[2048]{0:T(1024)S(1)} %fusion.25), kind=kCustom, calls=%fused_computation | custom fusion | bytes 16785408 | tf_op jit(solution)/shard_map/jit(_take)/gather | solution.py:23
  61.1 0.0 copy-done.4
  61.1 12.3 %fusion.3 = f32[2048,33]{0,1:T(8,128)} fusion(s32[2048,1024]{1,0:T(8,128)} %gather_fusion, f32[2048]{0:T(1024)S(1)} %gather_fusion.2, f32[2048]{0:T(1024)S(1)} %gather_fusion.1, pred[2048]{0:T(1024)(128)(4,1)S(1)} %compare_and_fusion, f32[1,1024]{1,0:T(1,128)S(1)} %bitcast.33, f32[32,1024]{1,0:T(8,128)S(1)} %add_convert_fusion), kind=kOutput, calls=%fused_computation.7 | convolution fusion | flops 838894592 | bytes 8812544 | tf_op jit(solution)/shard_map/dot_general | solution.py:29
  73.3 0.0 reduce-scatter.2.cloned.1.call-update
  73.4 9.3 %copy.22 = s32[1024,16,128]{2,0,1:T(8,128)} copy(s32[1024,16,128]{0,2,1:T(8,128)} %bitcast.27) | data formatting | bytes 16777216 | tf_op jit(solution)/shard_map/jit(_take)/gather | solution.py:23
  82.6 45.9 %reduce-scatter.2.cloned.1.call-done = f32[128,33]{0,1:T(8,128)} async-done(((f32[2048,33]{0,1:T(8,128)}), f32[128,33]{0,1:T(8,128)}) %reduce-scatter.2.cloned.1.call-update) | async-done | bytes 16912 | tf_op jit(solution)/shard_map/reduce_scatter | solution.py:28
  128.6 20.7 %all_gather.9 = f32[2048,33]{0,1:T(8,128)S(1)} all-gather(f32[128,33]{0,1:T(8,128)} %reduce-scatter.2.cloned.1.call-done), channel_id=1, replica_groups=mesh['grp'=2,'samp'=16] {'samp'}, dimensions={0}, use_global_device_ids=true | all-gather | bytes 287232 | tf_op jit(solution)/shard_map/all_gather | solution.py:39
  149.3 0.1 copy.28
  149.4 11.3 %fusion.18 = f32[16,33,1024]{2,1,0:T(8,128)S(1)} fusion(s32[1024,16,128]{2,0,1:T(8,128)} %copy.22, f32[16,128]{1,0:T(8,128)S(1)} %bitcast.31, f32[16,128]{1,0:T(8,128)S(1)} %bitcast.32, pred[16,128]{1,0:T(8,128)(4,1)S(1)} %fusion.31, f32[16,128,33]{1,0,2:T(8,128)S(1)} %slice_bitcast_fusion), kind=kOutput, calls=%fused_computation.21 | convolution fusion | flops 839401472 | bytes 10840064 | tf_op jit(solution)/shard_map/skm,kmr->krs/dot_general | solution.py:43
  160.7 1.3 copy.27
  161.9 0.0 copy-start.2
  162.0 3.1 %convolution_bitcast_fusion = f32[16,16,33]{0,1,2:T(8,128)S(1)} fusion(f32[16,33,1024]{2,0,1:T(8,128)S(1)} %copy.27), kind=kOutput, calls=%fused_computation.22 | convolution fusion | flops 103809024 | bytes 2196480 | tf_op jit(solution)/shard_map/krs,lrs->klr/dot_general | solution.py:46
  165.1 0.2 copy.26
  165.3 29.5 %all-gather = f32[256,16,33]{2,1,0:T(8,128)} all-gather(f32[16,16,33]{2,1,0:T(8,128)S(1)} %copy.26), channel_id=2, replica_groups=mesh['grp'=2,'samp'=16] {'samp'}, dimensions={0}, use_global_device_ids=true | all-gather | bytes 574464 | tf_op jit(solution)/shard_map/all_gather | solution.py:12
  194.8 1.8 reduce_sum.9
  196.6 0.7 broadcast_multiply_fusion.1
  197.2 0.0 copy-done.2
  (7 shorter events, 0.1 us)
Async XLA Ops:
  7.2 5.8 %copy-start = (f32[2048]{0:T(1024)S(1)}, f32[2048]{0:T(1024)}, u32[]{:S(2)}) copy-start(f32[2048]{0:T(1024)} %param.10) | copy-start | bytes 24580
  7.2 17.6 %copy-start.1 = (f32[2048]{0:T(1024)S(1)}, f32[2048]{0:T(1024)}, u32[]{:S(2)}) copy-start(f32[2048]{0:T(1024)} %param.9) | copy-start | bytes 24580
  7.2 121.4 %reduce-scatter.2.cloned.1.call-start = ((), (), s32[]{:S(2)}) async-start(), calls=%async_computation.1 | async-start | bytes 348160 | tf_op jit(solution)/shard_map/reduce_scatter | solution.py:28
  13.0 23.6 %copy-start.3 = (s32[32,1024]{1,0:T(8,128)S(1)}, s32[32,1024]{1,0:T(8,128)}, u32[]{:S(2)}) copy-start(s32[32,1024]{1,0:T(8,128)} %param.7) | copy-start | bytes 393220
  45.9 15.2 %copy-start.4 = (f32[1024]{0:T(1024)S(1)}, f32[1024]{0:T(1024)}, u32[]{:S(2)}) copy-start(f32[1024]{0:T(1024)} %param.8) | copy-start | bytes 12292
  161.9 35.3 %copy-start.2 = (f32[16,33,1024]{2,0,1:T(8,128)}, f32[16,33,1024]{2,0,1:T(8,128)S(1)}, u32[]{:S(2)}) copy-start(f32[16,33,1024]{2,0,1:T(8,128)S(1)} %copy.27) | copy-start | bytes 6488068
Sparse Core Ops, SparseCore 0:
  73.5 55.0 reduce-scatter.1
